TPU v7x, 32 devices: a whole 2x2x4 slice. The times are simulated.
32 devices in a mesh: seq: 4 (over y, x), res: 8 (over z, core).
Axes of the slice: x: 2, y: 2, z: 4, core: 2. Of those that a mesh axis runs over, the one named last changes fastest.
Arguments:
- alignment: float32 [256, 64, 256], P('seq', 'res'), may hold values from -100 to 100
- pair_features: float32 [64, 64, 128], P('seq', 'res'), may hold values from -100 to 100
- outer_gain: float32 [256], replicated, may hold values from 0.5 to 1.5
- w_outer_in: float32 [256, 64], replicated, may hold values from -0.375 to 0.375
- w_outer_out: float32 [1024, 128], replicated, may hold values from -0.1875 to 0.1875
- pair_gain: float32 [128], replicated, may hold values from 0.5 to 1.5
- w_bias: float32 [128, 8], replicated, may hold values from -30 to 30
- row_gain: float32 [256], replicated, may hold values from 0.5 to 1.5
- w_project: float32 [256, 1024], replicated, may hold values from -0.375 to 0.375
- w_output: float32 [256, 256], replicated, may hold values from -0.375 to 0.375
Outputs:
- alignment_out: float32 [256, 64, 256], P('seq', 'res')
- updated_pair_array: float32 [64, 64, 128], P('seq', 'res')
All inputs are finite; a program needn't handle non-finite values.
Results may differ from a plain program's by a relative error of at most 0.00018.
Values sent between devices are 32-bit elements; how exact they have to be, the bound alone decides.
A program may use at most 128 MiB of HBM per device.

v0:
```python
import jax
import jax.numpy as jnp
from jax import lax
from jax.sharding import PartitionSpec as P

precise = lax.Precision.HIGHEST


def layer_norm(values, scales):
    average = jnp.mean(values, axis=-1, keepdims=True)
    centered = values - average
    variance = jnp.mean(centered * centered, axis=-1, keepdims=True)
    return centered * lax.rsqrt(variance + 1e-05) * scales


def row_attention(sequence, bias_all, row_gain, w_project, w_output):
    residues, channels = sequence.shape
    head_count = bias_all.shape[0]
    head_size = channels // head_count
    normed_rows = layer_norm(sequence, row_gain)
    projected = jnp.dot(
        normed_rows, w_project, precision=precise, preferred_element_type=jnp.float32
    )
    query_map = projected[:, :channels].reshape(residues, head_count, head_size) * head_size ** (
        -0.5
    )
    key_map = projected[:, channels : 2 * channels].reshape(residues, head_count, head_size)
    value_map = projected[:, 2 * channels : 3 * channels].reshape(residues, head_count, head_size)
    gate_map = projected[:, 3 * channels :]
    scores = jnp.einsum("ihd,jhd->hij", query_map, key_map, precision=precise) + bias_all
    weights = jax.nn.softmax(scores, axis=-1)
    mixed_heads = jnp.einsum("hij,jhd->ihd", weights, value_map, precision=precise).reshape(
        residues, channels
    )
    gated_out = jax.nn.sigmoid(gate_map) * mixed_heads
    return sequence + jnp.dot(
        gated_out, w_output, precision=precise, preferred_element_type=jnp.float32
    )


def on_device(
    alignment,
    pair_features,
    outer_gain,
    w_outer_in,
    w_outer_out,
    pair_gain,
    w_bias,
    row_gain,
    w_project,
    w_output,
):
    sequence_local_count, residue_local_count, alignment_channel_count = alignment.shape
    row_block = pair_features.shape[0]
    sequence_group_list = lax.axis_size("res")
    seq_groups = lax.axis_size("seq")
    seq_total = sequence_local_count * seq_groups
    channels = w_outer_in.shape[1] // 2
    normed_rows = layer_norm(alignment, outer_gain)
    both_maps = jnp.einsum("src,cd->sdr", normed_rows, w_outer_in, precision=precise)
    left_maps = both_maps[:, :channels]
    right_maps = both_maps[:, channels:]
    left_all = lax.all_gather(left_maps, "res", axis=2, tiled=True)
    left_rows = lax.all_to_all(left_all, "seq", split_axis=2, concat_axis=0, tiled=True)
    product = jnp.einsum(
        "sxi,syj->ijxy",
        left_rows,
        lax.all_gather(right_maps, "seq", axis=0, tiled=True),
        precision=precise,
    )
    summed = product.reshape(row_block, residue_local_count, channels * channels)
    pair_update = jnp.einsum("ijk,kc->ijc", summed / seq_total, w_outer_out, precision=precise)
    updated_pair_array = pair_features + pair_update
    bias_tile = jnp.einsum(
        "ijc,ch->hij", layer_norm(updated_pair_array, pair_gain), w_bias, precision=precise
    )
    bias_rows = lax.all_gather(bias_tile, "res", axis=2, tiled=True)
    bias_all = lax.all_gather(bias_rows, "seq", axis=1, tiled=True)
    sequence_grouped_rows = alignment.reshape(
        sequence_group_list,
        sequence_local_count // sequence_group_list,
        residue_local_count,
        alignment_channel_count,
    )
    sequences = lax.all_to_all(
        sequence_grouped_rows, "res", split_axis=0, concat_axis=2, tiled=True
    )[0]
    updated = jax.vmap(row_attention, in_axes=(0, None, None, None, None))(
        sequences, bias_all, row_gain, w_project, w_output
    )
    attended = updated[None]
    returned_result = lax.all_to_all(attended, "res", split_axis=2, concat_axis=0, tiled=True)
    return (
        returned_result.reshape(sequence_local_count, residue_local_count, alignment_channel_count),
        updated_pair_array,
    )


def solution(mesh):
    in_specs = (
        P("seq", "res", None),
        P("seq", "res", None),
        P(),
        P(),
        P(),
        P(),
        P(),
        P(),
        P(),
        P(),
    )
    out_specs = (P("seq", "res", None), P("seq", "res", None))
    return jax.shard_map(
        on_device, mesh=mesh, in_specs=in_specs, out_specs=out_specs, check_vma=False
    )
```

profile of v0, /device:TPU:0, one launch (start us, length us, event | category | flops | bytes accessed | tf_op | source)
XLA Modules:
  0.0 148.9 jit_solution(3641051938862273192)
XLA Ops:
  0.6 1.3 reduce_sum.65
  1.9 1.3 multiply_reduce_fusion
  3.2 1.7 %convolution_bitcast_fusion = f32[64,64,8]{1,2,0:T(8,128)S(1)} fusion(f32[64,8,256]{2,1,0:T(8,128)} %param.10, f32[256]{0:T(256)} %param.12, f32[64,8]{1,0:T(8,128)S(1)} %add_rsqrt_fusion, f32[64,8]{1,0:T(8,128)S(1)} %broadcast_multiply_fusion, f32[256,64]{0,1:T(8,128)} %param.13), kind=kOutput, calls=%fused_computation.8 | convolution fusion | flops 101056512 | bytes 726016 | tf_op jit(solution)/shard_map/src,cd->sdr/dot_general | solution.py:60
  5.1 25.1 %all_gather.13 = f32[64,32,64]{1,2,0:T(8,128)S(1)} all-gather(f32[64,32,8]{1,2,0:T(8,128)S(1)} %get-tuple-element.5), channel_id=1, replica_groups=mesh['seq'=4,'res'=8] {'res'}, dimensions={2}, use_global_device_ids=true | all-gather | bytes 589824 | tf_op jit(solution)/shard_map/all_gather | solution.py:63
  30.2 2.1 %copy.39 = f32[64,32,64]{0,1,2:T(8,128)} copy(f32[64,32,64]{1,2,0:T(8,128)S(1)} %all_gather.13) | data formatting | bytes 1048576 | tf_op jit(solution)/shard_map/all_gather | solution.py:63
  32.3 2.7 %reshape.99 = f32[4,1,32768]{2,1,0:T(1,128)} reshape(f32[64,32,64]{2,1,0:T(8,128)} %bitcast.73) | data formatting | bytes 1048576
  35.0 3.7 %all-to-all-start.1 = ((f32[4,1,32768]{2,1,0:T(1,128)}), f32[4,1,32768]{2,1,0:T(1,128)S(1)}, u32[]{:S(2)}, u32[]{:S(2)}) async-start(f32[4,1,32768]{2,1,0:T(1,128)} %reshape.99), calls=%async_computation.1 | async-start | bytes 1048576 | tf_op jit(solution)/shard_map/all_to_all | solution.py:64
  38.7 18.5 %all_gather.12 = f32[256,32,8]{1,2,0:T(8,128)S(1)} all-gather(f32[64,32,8]{1,2,0:T(8,128)S(1)} %get-tuple-element.6), channel_id=1, replica_groups=mesh['seq'=4,'res'=8] {'seq'}, dimensions={0}, use_global_device_ids=true | all-gather | bytes 327680 | tf_op jit(solution)/shard_map/all_gather | solution.py:68
  57.6 4.3 %all-to-all-start = ((f32[8,8,8,256]{3,2,1,0:T(8,128)}), f32[8,8,8,256]{3,2,1,0:T(8,128)}, u32[]{:S(2)}, u32[]{:S(2)}) async-start(f32[8,8,8,256]{3,2,1,0:T(8,128)} %bitcast), calls=%async_computation | async-start | bytes 1048576 | tf_op jit(solution)/shard_map/all_to_all | solution.py:85
  62.5 2.1 %reduce.2 = f32[4,32768]{1,0:T(4,128)S(1)} reduce(f32[4,1,32768]{2,1,0:T(1,128)S(1)} %all-to-all-done.1, f32[]{:T(128)} %broadcast.97), dimensions={1}, to_apply=%all_to_all.38.reduce_sub_computation | reduce | bytes 1048580 | tf_op jit(solution)/shard_map/all_to_all | solution.py:64
  65.2 0.7 copy.59
  65.9 0.6 reshape.94
  66.5 3.2 %multiply_bitcast_fusion = f32[16,8,32,32]{2,1,0,3:T(8,128)} fusion(f32[256,32,8,1]{0,2,3,1:T(8,128)S(1)} %copy.49, f32[256,32,16,1]{0,1,2,3:T(8,128)S(1)} %reshape.94), kind=kOutput, calls=%fused_computation.3 | convolution fusion | flops 402784256 | bytes 1310720 | tf_op jit(solution)/shard_map/sxi,syj->ijxy/dot_general | solution.py:65
  69.7 2.3 %copy.42 = f32[16,8,32,32]{3,2,1,0:T(8,128)S(1)} copy(f32[16,8,32,32]{2,1,0,3:T(8,128)} %multiply_bitcast_fusion) | data formatting | bytes 1048576 | tf_op jit(solution)/shard_map/div | solution.py:72
  72.0 1.7 %div.50 = f32[16,8,1024]{2,1,0:T(8,128)} reshape(f32[16,8,32,32]{3,2,1,0:T(8,128)S(1)} %copy.42) | data formatting | bytes 1048576 | tf_op jit(solution)/shard_map/div | solution.py:72
  73.7 1.9 %fusion.41 = (f32[16,8]{1,0:T(8,128)S(1)}, f32[16,8,128]{2,1,0:T(8,128)S(1)}) fusion(f32[16,8,128]{2,1,0:T(8,128)S(1)} %copy-done.3, f32[16,8,1024]{2,1,0:T(8,128)} %div.50, f32[1024,128]{1,0:T(8,128)} %param.14), kind=kOutput, calls=%fused_computation.60 | convolution fusion | flops 201359232 | bytes 1180160 | tf_op jit(solution)/shard_map/ijk,kc->ijc/dot_general | solution.py:72
  76.1 14.9 %all_gather.14 = f32[8,16,64]{0,2,1:T(8,128)S(1)} all-gather(f32[8,16,8]{0,2,1:T(8,128)S(1)} %convolution_bitcast_fusion.1), channel_id=1, replica_groups=mesh['seq'=4,'res'=8] {'res'}, dimensions={2}, use_global_device_ids=true | all-gather | bytes 36864 | tf_op jit(solution)/shard_map/all_gather | solution.py:77
  91.2 8.4 %all_gather.15 = f32[8,64,64]{2,0,1:T(8,128)S(1)} all-gather(f32[8,16,64]{2,0,1:T(8,128)S(1)} %copy.43), channel_id=1, replica_groups=mesh['seq'=4,'res'=8] {'seq'}, dimensions={1}, use_global_device_ids=true | all-gather | bytes 163840 | tf_op jit(solution)/shard_map/all_gather | solution.py:78
  99.8 1.2 bitcast_reduce_fusion
  101.1 1.3 multiply_reduce_fusion.1
  102.5 2.9 %fusion.4 = f32[8,64,1024]{2,1,0:T(8,128)S(1)} fusion(f32[256,1024]{1,0:T(8,128)S(1)} %copy-done, f32[256]{0:T(256)S(1)} %copy-done.4, f32[8,64]{1,0:T(8,128)S(1)} %rsqrt.28, f32[8,64]{1,0:T(8,128)S(1)} %div.42, f32[8,8,8,256]{3,2,1,0:T(8,128)} %all-to-all-done), kind=kOutput, calls=%fused_computation.11 | convolution fusion | flops 1611005952 | bytes 3675136 | tf_op jit(solution)/shard_map/vmap()/dot_general | solution.py:21
  105.5 1.2 fusion.39
  106.7 2.4 %copy.38 = f32[8,64,256]{1,2,0:T(8,128)} copy(f32[8,64,256]{2,1,0:T(8,128)} %get-tuple-element.2) | data formatting | bytes 1048576 | tf_op jit(solution)/shard_map/vmap()/slice | solution.py:27
  109.1 2.4 %copy.37 = f32[8,64,256]{1,2,0:T(8,128)} copy(f32[8,64,256]{2,1,0:T(8,128)} %get-tuple-element.3) | data formatting | bytes 1048576 | tf_op jit(solution)/shard_map/vmap()/mul | solution.py:24
  111.5 2.4 %copy.36 = f32[8,64,256]{1,2,0:T(8,128)} copy(f32[8,64,256]{2,1,0:T(8,128)} %get-tuple-element.4) | data formatting | bytes 1048576 | tf_op jit(solution)/shard_map/vmap()/slice | solution.py:28
  113.8 5.1 %add_reduce_fusion = (f32[8,8,64]{2,1,0:T(8,128)S(1)}, f32[8,8,64,64]{2,3,1,0:T(8,128)S(1)}) fusion(f32[8,64,64]{1,2,0:T(8,128)S(1)} %copy.44, f32[8,64,8,32]{1,3,2,0:T(8,128)} %bitcast.72, f32[8,64,8,32]{1,3,2,0:T(8,128)} %bitcast.71), kind=kOutput, calls=%fused_computation.4 | convolution fusion | flops 101183488 | bytes 2244608 | tf_op jit(solution)/shard_map/vmap(ihd,jhd->hij)/dot_general | solution.py:30
  119.5 0.7 copy-done.1
  120.2 3.3 %fusion = f32[8,8,32,64]{3,2,1,0:T(8,128)} fusion(f32[8,64,8,32]{1,3,2,0:T(8,128)S(1)} %bitcast.78, f32[8,8,64,64]{2,3,1,0:T(8,128)S(1)} %get-tuple-element.10, f32[8,8,64]{2,1,0:T(8,128)S(1)} %fusion.2, f32[8,8,64]{2,1,0:T(8,128)S(1)} %get-tuple-element.9, f32[8,64,64]{1,2,0:T(8,128)S(1)} %copy.44), kind=kOutput, calls=%fused_computation | convolution fusion | flops 101449728 | bytes 2260992 | tf_op jit(solution)/shard_map/vmap(hij,jhd->ihd)/dot_general | solution.py:32
  123.5 2.3 %copy.46 = f32[8,64,256]{2,1,0:T(8,128)} copy(f32[8,64,256]{1,2,0:T(8,128)} %bitcast.79) | data formatting | bytes 1048576 | tf_op jit(solution)/shard_map/vmap()/reshape | solution.py:32
  125.8 1.9 %fusion.3 = f32[1,8,64,256]{3,2,1,0:T(8,128)S(1)} fusion(f32[8,64,256]{2,1,0:T(8,128)} %copy.46, f32[8,64,1024]{2,1,0:T(8,128)S(1)} %fusion.4, f32[256,256]{1,0:T(8,128)} %param.19, f32[8,8,8,256]{3,2,1,0:T(8,128)} %all-to-all-done), kind=kOutput, calls=%fused_computation.7 | convolution fusion | flops 403308544 | bytes 2359296 | tf_op jit(solution)/shard_map/vmap()/dot_general | solution.py:36
  128.1 19.8 %all_to_all.48 = f32[1,8,64,256]{3,1,0,2:T(8,128)S(1)} all-to-all(f32[1,8,64,256]{3,1,0,2:T(8,128)S(1)} %copy.47), channel_id=1, replica_groups=mesh['seq'=4,'res'=8] {'res'}, dimensions={2} | all-to-all | bytes 1048576 | tf_op jit(solution)/shard_map/all_to_all | solution.py:92
  148.0 1.0 copy.48
  (35 shorter events, 3.4 us)
Async XLA Ops:
  0.6 101.9 %copy-start = (f32[256,1024]{1,0:T(8,128)S(1)}, f32[256,1024]{1,0:T(8,128)}, u32[]{:S(2)}) copy-start(f32[256,1024]{1,0:T(8,128)} %param.18) | copy-start | bytes 3145732
  35.0 22.6 %all-to-all-start.1 = ((f32[4,1,32768]{2,1,0:T(1,128)}), f32[4,1,32768]{2,1,0:T(1,128)S(1)}, u32[]{:S(2)}, u32[]{:S(2)}) async-start(f32[4,1,32768]{2,1,0:T(1,128)} %reshape.99), calls=%async_computation.1 | async-start | bytes 1048576 | tf_op jit(solution)/shard_map/all_to_all | solution.py:64
  57.6 42.2 %all-to-all-start = ((f32[8,8,8,256]{3,2,1,0:T(8,128)}), f32[8,8,8,256]{3,2,1,0:T(8,128)}, u32[]{:S(2)}, u32[]{:S(2)}) async-start(f32[8,8,8,256]{3,2,1,0:T(8,128)} %bitcast), calls=%async_computation | async-start | bytes 1048576 | tf_op jit(solution)/shard_map/all_to_all | solution.py:85
  71.9 1.8 %copy-start.3 = (f32[16,8,128]{2,1,0:T(8,128)S(1)}, f32[16,8,128]{2,1,0:T(8,128)}, u32[]{:S(2)}) copy-start(f32[16,8,128]{2,1,0:T(8,128)} %param.11) | copy-start | bytes 196612
  71.9 3.9 %copy-start.5 = (f32[128,8]{0,1:T(8,128)S(1)}, f32[128,8]{0,1:T(8,128)}, u32[]{:S(2)}) copy-start(f32[128,8]{0,1:T(8,128)} %param.16) | copy-start | bytes 12292
  71.9 3.9 %copy-start.6 = (f32[128]{0:T(128)S(1)}, f32[128]{0:T(128)}, u32[]{:S(2)}) copy-start(f32[128]{0:T(128)} %param.15) | copy-start | bytes 1540
  75.6 29.8 %copy-start.2 = (f32[16,8,128]{2,1,0:T(8,128)}, f32[16,8,128]{2,1,0:T(8,128)S(1)}, u32[]{:S(2)}) copy-start(f32[16,8,128]{2,1,0:T(8,128)S(1)} %get-tuple-element.8) | copy-start | bytes 196612
  75.6 26.9 %copy-start.4 = (f32[256]{0:T(256)S(1)}, f32[256]{0:T(256)}, u32[]{:S(2)}) copy-start(f32[256]{0:T(256)} %param.17) | copy-start | bytes 3076
  118.9 1.2 copy-start.1
where the time goes:
time: 150 us; the launch traced here: 149 us
  blocking collectives  86.8 us (58%)
  local copies, waits for them, and re-layouts  23.6 us (16%)
  matrix products  20.3 us (14%)
  other arithmetic  9.14 us (6%)
  starting transfers between devices  8.05 us (5%)
    all_gather x1, blocking collectives, on_device(): left_all = lax.all_gather(left_maps, 'res', axis=2, tiled=True)  25.1 us
    all_to_all x1, blocking collectives, on_device(): lax.all_to_all(attended, 'res', split_axis=2, concat_axis=0, tiled=True)  19.8 us
    all_gather x1, blocking collectives, on_device(): lax.all_gather(right_maps, 'seq', axis=0, tiled=True)  18.5 us
    all_gather x1, blocking collectives, on_device(): bias_rows = lax.all_gather(bias_tile, 'res', axis=2, tiled=True)  14.9 us
    all_gather x1, blocking collectives, on_device(): bias_all = lax.all_gather(bias_rows, 'seq', axis=1, tiled=True)  8.4 us
    dot_general x1, matrix products, row_attention(): jnp.einsum('ihd,jhd->hij', query_map, key_map, precision=precise) + bias_all  5.09 us
    all_to_all x1, starting transfers between devices, on_device(): lax.all_to_all(sequence_grouped_rows, 'res', split_axis=0, concat_axis=2,...  4.34 us
    div x2, local copies, waits for them, and re-layouts, on_device(): summed / seq_total  4 us
  transfers between devices with their start and end apart: 2, of which 0 were waited for; matrix products, arithmetic and copies ran while one was open for 10% of the time, Pallas kernels for 0%

commit v1 on v0

--- a/solution.py
+++ b/solution.py
@@ -4,6 +4,22 @@
 from jax.sharding import PartitionSpec as P
 
 precise = lax.Precision.HIGHEST
+
+
+def choose_runs(local_x, dim_at, frame):
+    low, raw_out, before = (lax.axis_size("seq"), lax.axis_index("seq"), local_x.shape[dim_at])
+    sheets = list(map(lambda pp: (pp, (pp + 1) % low), range(low)))
+    made = list(map(lambda pp: (pp, (pp - 1) % low), range(low)))
+    val2 = low // 2
+    r_now = piece_next = local_x
+    piece_now = frame(local_x, raw_out * before)
+    for p in range(1, val2 + 1):
+        r_now = lax.ppermute(r_now, axis_name="seq", perm=sheets)
+        if p < low - val2:
+            piece_next = lax.ppermute(piece_next, axis_name="seq", perm=made)
+            piece_now = piece_now + frame(piece_next, (raw_out + p) % low * before)
+        piece_now = piece_now + frame(r_now, (raw_out - p) % low * before)
+    return piece_now
 
 
 def layer_norm(values, scales):
@@ -62,11 +78,15 @@
     right_maps = both_maps[:, channels:]
     left_all = lax.all_gather(left_maps, "res", axis=2, tiled=True)
     left_rows = lax.all_to_all(left_all, "seq", split_axis=2, concat_axis=0, tiled=True)
-    product = jnp.einsum(
-        "sxi,syj->ijxy",
-        left_rows,
-        lax.all_gather(right_maps, "seq", axis=0, tiled=True),
-        precision=precise,
+    product = choose_runs(
+        right_maps,
+        0,
+        lambda shard, offset: jnp.einsum(
+            "sxi,syj->ijxy",
+            lax.dynamic_slice_in_dim(left_rows, offset, shard.shape[0], axis=0),
+            shard,
+            precision=precise,
+        ),
     )
     summed = product.reshape(row_block, residue_local_count, channels * channels)
     pair_update = jnp.einsum("ijk,kc->ijc", summed / seq_total, w_outer_out, precision=precise)

time: 150 us -> 163 us (1.087)
  blocking collectives: 86.8 us -> 69.6 us
  matrix products: 20.3 us -> 33.5 us
  waiting for transfers between devices: 0.01 us -> 13.1 us
  starting transfers between devices: 8.05 us -> 11 us
    all_gather x1 -> x0, blocking collectives: 18.5 us -> none  [on_device(): lax.all_gather(right_maps, 'seq', axis=0, tiled=True)]
    dot_general x1 -> x4, matrix products: 3.15 us -> 17.5 us  [on_device(): jnp.einsum('sxi,syj->ijxy', lax.dynamic_slice_in_dim(left_rows, offset, s...]
    ppermute x0 -> x3, waiting for transfers between devices: none -> 13.1 us  [the longest x2 13.1 us: choose_runs(): r_now = lax.ppermute(r_now, axis_name='seq', perm=sheets)]
    ppermute x0 -> x3, starting transfers between devices: none -> 2.95 us  [the longest x2 2.03 us: choose_runs(): r_now = lax.ppermute(r_now, axis_name='seq', perm=sheets)]
    unnamed x16 -> x20, local copies, waits for them, and re-layouts: 3.91 us -> 3.91 us
  transfers between devices with their start and end apart: 2 -> 5, of which waited for: 0 -> 1; matrix products, arithmetic and copies ran while one was open for 10% -> 17% of each run, Pallas kernels for 0% -> 0%
where the time goes in v1:
time: 163 us; the launch traced here: 162 us
  blocking collectives  69.6 us (43%)
  matrix products  33.5 us (21%)
  local copies, waits for them, and re-layouts  24.4 us (15%)
  waiting for transfers between devices  13.1 us (8%)
  starting transfers between devices  11 us (7%)
  other arithmetic  9.14 us (6%)
    all_gather x1, blocking collectives, on_device(): left_all = lax.all_gather(left_maps, 'res', axis=2, tiled=True)  25.1 us
    all_to_all x1, blocking collectives, on_device(): lax.all_to_all(attended, 'res', split_axis=2, concat_axis=0, tiled=True)  19.8 us
    dot_general x4, matrix products, on_device(): jnp.einsum('sxi,syj->ijxy', lax.dynamic_slice_in_dim(left_rows, offset, s...  17.5 us
    all_gather x1, blocking collectives, on_device(): bias_rows = lax.all_gather(bias_tile, 'res', axis=2, tiled=True)  14.9 us
    ppermute x2, waiting for transfers between devices, choose_runs(): r_now = lax.ppermute(r_now, axis_name='seq', perm=sheets)  13.1 us
    all_gather x1, blocking collectives, on_device(): bias_all = lax.all_gather(bias_rows, 'seq', axis=1, tiled=True)  9.75 us
    dot_general x1, matrix products, row_attention(): jnp.einsum('ihd,jhd->hij', query_map, key_map, precision=precise) + bias_all  5.09 us
    div x2, local copies, waits for them, and re-layouts, on_device(): summed / seq_total  4.38 us
  transfers between devices with their start and end apart: 5, of which 1 were waited for; matrix products, arithmetic and copies ran while one was open for 17% of the time, Pallas kernels for 0%

profile of v1, /device:TPU:0, one launch (start us, length us, event | category | flops | bytes accessed | tf_op | source)
XLA Modules:
  0.0 161.7 jit_solution(4749588379017308565)
XLA Ops:
  0.6 1.3 reduce_sum.65
  1.9 1.3 multiply_reduce_fusion
  3.2 1.7 %convolution_bitcast_fusion = f32[64,64,8]{1,2,0:T(8,128)S(1)} fusion(f32[64,8,256]{2,1,0:T(8,128)} %param.10, f32[256]{0:T(256)} %param.12, f32[64,8]{1,0:T(8,128)S(1)} %add_rsqrt_fusion, f32[64,8]{1,0:T(8,128)S(1)} %broadcast_multiply_fusion, f32[256,64]{0,1:T(8,128)} %param.13), kind=kOutput, calls=%fused_computation.8 | convolution fusion | flops 101056512 | bytes 726016 | tf_op jit(solution)/shard_map/src,cd->sdr/dot_general | solution.py:76
  5.8 25.1 %all_gather.9 = f32[64,32,64]{1,2,0:T(8,128)S(1)} all-gather(f32[64,32,8]{1,2,0:T(8,128)S(1)} %get-tuple-element.6), channel_id=1, replica_groups=mesh['seq'=4,'res'=8] {'res'}, dimensions={2}, use_global_device_ids=true | all-gather | bytes 589824 | tf_op jit(solution)/shard_map/all_gather | solution.py:79
  30.9 2.1 %copy.45 = f32[64,32,64]{0,1,2:T(8,128)} copy(f32[64,32,64]{1,2,0:T(8,128)S(1)} %all_gather.9) | data formatting | bytes 1048576 | tf_op jit(solution)/shard_map/all_gather | solution.py:79
  33.0 2.7 %reshape.104 = f32[4,1,32768]{2,1,0:T(1,128)} reshape(f32[64,32,64]{2,1,0:T(8,128)} %bitcast.87) | data formatting | bytes 1048576
  35.7 3.7 %all-to-all-start.1 = ((f32[4,1,32768]{2,1,0:T(1,128)}), f32[4,1,32768]{2,1,0:T(1,128)S(1)}, u32[]{:S(2)}, u32[]{:S(2)}) async-start(f32[4,1,32768]{2,1,0:T(1,128)} %reshape.104), calls=%async_computation.1 | async-start | bytes 1048576 | tf_op jit(solution)/shard_map/all_to_all | solution.py:80
  39.4 2.0 %collective-permute-start.1 = (f32[64,32,8]{1,2,0:T(8,128)}, f32[64,32,8]{1,2,0:T(8,128)}, u32[]{:S(2)}, u32[]{:S(2)}) collective-permute-start(f32[64,32,8]{1,2,0:T(8,128)} %get-tuple-element.7), channel_id=1, source_target_pairs={{0,8},{8,16},{16,24},{24,0},{1,9},{9,17},{17,25},{25,1},{2,10},{10... | collective-permute-start | bytes 196616 | tf_op jit(solution)/shard_map/ppermute | solution.py:17
  42.4 13.1 %collective-permute-done.1 = f32[64,32,8]{1,2,0:T(8,128)} collective-permute-done((f32[64,32,8]{1,2,0:T(8,128)}, f32[64,32,8]{1,2,0:T(8,128)}, u32[]{:S(2)}, u32[]{:S(2)}) %collective-permute-start.1) | collective-permute-done | bytes 65568 | tf_op jit(solution)/shard_map/ppermute | solution.py:17
  55.5 4.3 %all-to-all-start = ((f32[8,8,8,256]{3,2,1,0:T(8,128)}), f32[8,8,8,256]{3,2,1,0:T(8,128)}, u32[]{:S(2)}, u32[]{:S(2)}) async-start(f32[8,8,8,256]{3,2,1,0:T(8,128)} %bitcast), calls=%async_computation | async-start | bytes 1048576 | tf_op jit(solution)/shard_map/all_to_all | solution.py:105
  60.3 2.1 %reduce.2 = f32[4,32768]{1,0:T(4,128)S(1)} reduce(f32[4,1,32768]{2,1,0:T(1,128)S(1)} %all-to-all-done.1, f32[]{:T(128)} %broadcast.100), dimensions={1}, to_apply=%all_to_all.38.reduce_sub_computation | reduce | bytes 1048580 | tf_op jit(solution)/shard_map/all_to_all | solution.py:80
  64.3 4.7 %fusion.25 = f32[32,8,32,16]{2,0,3,1:T(8,128)S(1)} fusion(f32[64,32,8,1]{1,2,0,3:T(8,128)} %bitcast.17, f32[256,32,16]{0,1,2:T(8,128)S(1)} %all_to_all.41, s32[]{:T(128)S(6)} %select_n.31), kind=kOutput, calls=%fused_computation.36 | convolution fusion | flops 100663296 | bytes 851972 | tf_op jit(solution)/shard_map/sxi,syj->ijxy/dot_general | solution.py:84
  69.0 4.5 %fusion.28 = f32[32,8,32,16]{2,0,3,1:T(8,128)S(1)} fusion(f32[64,32,8,1]{1,2,0,3:T(8,128)} %bitcast.15, f32[256,32,16]{0,1,2:T(8,128)S(1)} %all_to_all.41, s32[]{:T(128)S(6)} %select_n.29), kind=kOutput, calls=%fused_computation.39 | convolution fusion | flops 100663296 | bytes 851972 | tf_op jit(solution)/shard_map/sxi,syj->ijxy/dot_general | solution.py:84
  73.5 3.7 %fusion.31 = f32[32,8,32,16]{2,0,3,1:T(8,128)S(1)} fusion(f32[64,32,8,1]{1,2,0,3:T(8,128)S(1)} %get-tuple-element.5, f32[256,32,16]{0,1,2:T(8,128)S(1)} %all_to_all.41, s32[]{:T(128)S(6)} %select_n.27), kind=kOutput, calls=%fused_computation.42 | convolution fusion | flops 100663296 | bytes 1048580 | tf_op jit(solution)/shard_map/sxi,syj->ijxy/dot_general | solution.py:84
  77.3 4.7 %multiply_bitcast_fusion = f32[16,8,32,32]{2,3,0,1:T(8,128)S(1)} fusion(f32[32,8,32,16]{2,0,3,1:T(8,128)S(1)} %fusion.25, f32[32,8,32,16]{2,0,3,1:T(8,128)S(1)} %fusion.31, f32[32,8,32,16]{2,0,3,1:T(8,128)S(1)} %fusion.28, f32[64,32,8,1]{1,2,0,3:T(8,128)} %bitcast.19, f32[256,32,16]{0,1,2:T(8,128)} %copy-done.1, s32[]{:T(128)S(6)} %select_n.33), kind=kOutput, calls=%fused_computation.3 | convolution fusion | flops 101187584 | bytes 2621444 | tf_op jit(solution)/shard_map/sxi,syj->ijxy/dot_general | solution.py:84
  81.9 1.9 %copy.51 = f32[16,8,32,32]{3,2,1,0:T(8,128)} copy(f32[16,8,32,32]{2,3,0,1:T(8,128)S(1)} %multiply_bitcast_fusion) | data formatting | bytes 1048576 | tf_op jit(solution)/shard_map/div | solution.py:92
  83.8 2.5 %div.50 = f32[16,8,1024]{2,1,0:T(8,128)S(1)} reshape(f32[16,8,32,32]{3,2,1,0:T(8,128)} %copy.51) | data formatting | bytes 1048576 | tf_op jit(solution)/shard_map/div | solution.py:92
  87.6 14.9 %all_gather.10 = f32[8,16,64]{0,2,1:T(8,128)S(1)} all-gather(f32[8,16,8]{0,2,1:T(8,128)S(1)} %convolution_bitcast_fusion.1), channel_id=1, replica_groups=mesh['seq'=4,'res'=8] {'res'}, dimensions={2}, use_global_device_ids=true | all-gather | bytes 36864 | tf_op jit(solution)/shard_map/all_gather | solution.py:97
  102.7 9.8 %all_gather.11 = f32[8,64,64]{2,0,1:T(8,128)S(1)} all-gather(f32[8,16,64]{2,0,1:T(8,128)S(1)} %copy.52), channel_id=1, replica_groups=mesh['seq'=4,'res'=8] {'seq'}, dimensions={1}, use_global_device_ids=true | all-gather | bytes 163840 | tf_op jit(solution)/shard_map/all_gather | solution.py:98
  112.6 1.2 bitcast_reduce_fusion
  113.8 1.3 multiply_reduce_fusion.1
  115.3 2.9 %fusion.4 = f32[8,64,1024]{2,1,0:T(8,128)S(1)} fusion(f32[256,1024]{1,0:T(8,128)S(1)} %copy-done, f32[256]{0:T(256)S(1)} %copy-done.6, f32[8,64]{1,0:T(8,128)S(1)} %rsqrt.28, f32[8,64]{1,0:T(8,128)S(1)} %div.42, f32[8,8,8,256]{3,2,1,0:T(8,128)} %all-to-all-done), kind=kOutput, calls=%fused_computation.11 | convolution fusion | flops 1611005952 | bytes 3675136 | tf_op jit(solution)/shard_map/vmap()/dot_general | solution.py:37
  118.3 1.2 fusion.58
  119.5 2.4 %copy.43 = f32[8,64,256]{1,2,0:T(8,128)} copy(f32[8,64,256]{2,1,0:T(8,128)} %get-tuple-element.3) | data formatting | bytes 1048576 | tf_op jit(solution)/shard_map/vmap()/mul | solution.py:40
  121.9 2.4 %copy.44 = f32[8,64,256]{1,2,0:T(8,128)} copy(f32[8,64,256]{2,1,0:T(8,128)} %get-tuple-element.2) | data formatting | bytes 1048576 | tf_op jit(solution)/shard_map/vmap()/slice | solution.py:43
  124.2 2.4 %copy.42 = f32[8,64,256]{1,2,0:T(8,128)} copy(f32[8,64,256]{2,1,0:T(8,128)} %get-tuple-element.4) | data formatting | bytes 1048576 | tf_op jit(solution)/shard_map/vmap()/slice | solution.py:44
  126.6 5.1 %add_reduce_fusion = (f32[8,8,64]{2,1,0:T(8,128)S(1)}, f32[8,8,64,64]{2,3,1,0:T(8,128)S(1)}) fusion(f32[8,64,64]{1,2,0:T(8,128)S(1)} %copy.53, f32[8,64,8,32]{1,3,2,0:T(8,128)} %bitcast.85, f32[8,64,8,32]{1,3,2,0:T(8,128)} %bitcast.86), kind=kOutput, calls=%fused_computation.4 | convolution fusion | flops 101183488 | bytes 2244608 | tf_op jit(solution)/shard_map/vmap(ihd,jhd->hij)/dot_general | solution.py:46
  133.0 3.3 %fusion = f32[8,8,32,64]{3,2,1,0:T(8,128)} fusion(f32[8,64,8,32]{1,3,2,0:T(8,128)S(1)} %bitcast.91, f32[8,8,64,64]{2,3,1,0:T(8,128)S(1)} %get-tuple-element.11, f32[8,8,64]{2,1,0:T(8,128)S(1)} %fusion.2, f32[8,8,64]{2,1,0:T(8,128)S(1)} %get-tuple-element.10, f32[8,64,64]{1,2,0:T(8,128)S(1)} %copy.53), kind=kOutput, calls=%fused_computation | convolution fusion | flops 101449728 | bytes 2260992 | tf_op jit(solution)/shard_map/vmap(hij,jhd->ihd)/dot_general | solution.py:48
  136.3 2.3 %copy.55 = f32[8,64,256]{2,1,0:T(8,128)} copy(f32[8,64,256]{1,2,0:T(8,128)} %bitcast.92) | data formatting | bytes 1048576 | tf_op jit(solution)/shard_map/vmap()/reshape | solution.py:48
  138.6 1.9 %fusion.3 = f32[1,8,64,256]{3,2,1,0:T(8,128)S(1)} fusion(f32[8,64,256]{2,1,0:T(8,128)} %copy.55, f32[8,64,1024]{2,1,0:T(8,128)S(1)} %fusion.4, f32[256,256]{1,0:T(8,128)} %param.19, f32[8,8,8,256]{3,2,1,0:T(8,128)} %all-to-all-done), kind=kOutput, calls=%fused_computation.7 | convolution fusion | flops 403308544 | bytes 2359296 | tf_op jit(solution)/shard_map/vmap()/dot_general | solution.py:52
  140.9 19.8 %all_to_all.48 = f32[1,8,64,256]{3,1,0,2:T(8,128)S(1)} all-to-all(f32[1,8,64,256]{3,1,0,2:T(8,128)S(1)} %copy.56), channel_id=1, replica_groups=mesh['seq'=4,'res'=8] {'res'}, dimensions={2} | all-to-all | bytes 1048576 | tf_op jit(solution)/shard_map/all_to_all | solution.py:112
  160.8 1.0 copy.57
  (46 shorter events, 7.4 us)
Async XLA Ops:
  0.6 114.7 %copy-start = (f32[256,1024]{1,0:T(8,128)S(1)}, f32[256,1024]{1,0:T(8,128)}, u32[]{:S(2)}) copy-start(f32[256,1024]{1,0:T(8,128)} %param.18) | copy-start | bytes 3145732
  35.7 19.8 %all-to-all-start.1 = ((f32[4,1,32768]{2,1,0:T(1,128)}), f32[4,1,32768]{2,1,0:T(1,128)S(1)}, u32[]{:S(2)}, u32[]{:S(2)}) async-start(f32[4,1,32768]{2,1,0:T(1,128)} %reshape.104), calls=%async_computation.1 | async-start | bytes 1048576 | tf_op jit(solution)/shard_map/all_to_all | solution.py:80
  39.4 16.1 %collective-permute-start.1 = (f32[64,32,8]{1,2,0:T(8,128)}, f32[64,32,8]{1,2,0:T(8,128)}, u32[]{:S(2)}, u32[]{:S(2)}) collective-permute-start(f32[64,32,8]{1,2,0:T(8,128)} %get-tuple-element.7), channel_id=1, source_target_pairs={{0,8},{8,16},{16,24},{24,0},{1,9},{9,17},{17,25},{25,1},{2,10},{10... | collective-permute-start | bytes 196616 | tf_op jit(solution)/shard_map/ppermute | solution.py:17
  41.4 27.6 %collective-permute-start = (f32[64,32,8]{1,2,0:T(8,128)}, f32[64,32,8]{1,2,0:T(8,128)}, u32[]{:S(2)}, u32[]{:S(2)}) collective-permute-start(f32[64,32,8]{1,2,0:T(8,128)} %get-tuple-element.7), channel_id=1, source_target_pairs={{0,24},{8,0},{16,8},{24,16},{1,25},{9,1},{17,9},{25,17},{2,26},{10... | collective-permute-start | bytes 196616 | tf_op jit(solution)/shard_map/ppermute | solution.py:19
  55.5 21.8 %collective-permute-start.2 = (f32[64,32,8]{1,2,0:T(8,128)}, f32[64,32,8]{1,2,0:T(8,128)}, u32[]{:S(2)}, u32[]{:S(2)}) collective-permute-start(f32[64,32,8]{1,2,0:T(8,128)} %collective-permute-done.1), channel_id=1, source_target_pairs={{0,8},{8,16},{16,24},{24,0},{1,9},{9,17},{17,25},{25,1},{2,10},{10... | collective-permute-start | bytes 196616 | tf_op jit(solution)/shard_map/ppermute | solution.py:17
  55.5 57.1 %all-to-all-start = ((f32[8,8,8,256]{3,2,1,0:T(8,128)}), f32[8,8,8,256]{3,2,1,0:T(8,128)}, u32[]{:S(2)}, u32[]{:S(2)}) async-start(f32[8,8,8,256]{3,2,1,0:T(8,128)} %bitcast), calls=%async_computation | async-start | bytes 1048576 | tf_op jit(solution)/shard_map/all_to_all | solution.py:105
  64.3 9.2 %copy-start.1 = (f32[256,32,16]{0,1,2:T(8,128)}, f32[256,32,16]{0,1,2:T(8,128)S(1)}, u32[]{:S(2)}) copy-start(f32[256,32,16]{0,1,2:T(8,128)S(1)} %all_to_all.41) | copy-start | bytes 1572868
  83.8 2.5 %copy-start.3 = (f32[1024,128]{1,0:T(8,128)S(1)}, f32[1024,128]{1,0:T(8,128)}, u32[]{:S(2)}) copy-start(f32[1024,128]{1,0:T(8,128)} %param.14) | copy-start | bytes 1572868
  83.8 2.5 %copy-start.5 = (f32[16,8,128]{2,1,0:T(8,128)S(1)}, f32[16,8,128]{2,1,0:T(8,128)}, u32[]{:S(2)}) copy-start(f32[16,8,128]{2,1,0:T(8,128)} %param.11) | copy-start | bytes 196612
  83.8 3.5 %copy-start.7 = (f32[128,8]{0,1:T(8,128)S(1)}, f32[128,8]{0,1:T(8,128)}, u32[]{:S(2)}) copy-start(f32[128,8]{0,1:T(8,128)} %param.16) | copy-start | bytes 12292
  83.8 3.5 %copy-start.8 = (f32[128]{0:T(128)S(1)}, f32[128]{0:T(128)}, u32[]{:S(2)}) copy-start(f32[128]{0:T(128)} %param.15) | copy-start | bytes 1540
  87.1 31.2 %copy-start.4 = (f32[16,8,128]{2,1,0:T(8,128)}, f32[16,8,128]{2,1,0:T(8,128)S(1)}, u32[]{:S(2)}) copy-start(f32[16,8,128]{2,1,0:T(8,128)S(1)} %get-tuple-element.9) | copy-start | bytes 196612
  87.1 28.3 %copy-start.6 = (f32[256]{0:T(256)S(1)}, f32[256]{0:T(256)}, u32[]{:S(2)}) copy-start(f32[256]{0:T(256)} %param.17) | copy-start | bytes 3076
  131.7 1.2 copy-start.2
